TPU v7x, 512 devices: a whole 4x8x8 slice. The times are simulated.
512 devices in a mesh: inp: 128 (over y, z, core), vis: 4 (over x).
Axes of the slice: x: 4, y: 8, z: 8, core: 2. Of those that a mesh axis runs over, the one named last changes fastest.
Arguments:
- samples: bfloat16 [128, 2048, 2048], P('vis', 'inp'), may hold values from -6 to 6
- history: bfloat16 [3, 2048, 2048], P(None, 'inp'), may hold values from -6 to 6
- fir_taps: float32 [4, 2048], replicated, may hold values from -3 to 3
- kept_channels: int32 [128], replicated, may hold values from 0 to 1023, as said below
Outputs:
- visibility: bfloat16 [128, 2048, 2048], P('inp', 'vis')
Inputs may be any that keep to these rules, and one draw needn't show every extreme that they name: `kept_channels`: 128 distinct channel numbers in no particular order; channels 0 and 1023 are always among them.
All inputs are finite; a program needn't handle non-finite values.
Results may differ from a plain program's by a relative error of at most 0.0078.
Values may be sent and summed in bfloat16 or wider, within the bound.
A program may use at most 64 MiB of HBM per device.

v0:
```python
from functools import partial
import math
import jax
import jax.numpy as jnp
from jax import lax
from jax.sharding import PartitionSpec as P

TAPS = 4
CH_DEV = 1


def shifted(value, axis, steps):
    count = lax.axis_size(axis)
    initial, last = (max(0, -steps), min(count, count - steps))
    return lax.ppermute(value, axis, [(source, source + steps) for source in range(initial, last)])


def make_table(kept_channels, sample_count):
    positions = jnp.arange(sample_count, dtype=jnp.int32)
    products = kept_channels[:, None] * positions[None, :] % sample_count
    angles = products.astype(jnp.float32) * (2.0 * math.pi / sample_count)
    norm_scale = 1.0 / math.sqrt(sample_count)
    table = jnp.concatenate([jnp.cos(angles) * norm_scale, -jnp.sin(angles) * norm_scale], axis=0)
    return table.astype(jnp.bfloat16)


def add_frames(running, shard_piece, offset, vis_index, row_count):
    real_part = shard_piece[0]
    imag_part = shard_piece[1]
    stacked = jnp.concatenate([real_part, imag_part], axis=1)
    rotated = jnp.concatenate([-imag_part, real_part], axis=1)
    row_block = lax.dynamic_slice_in_dim(stacked, vis_index * row_count, row_count, 2)
    input_total = stacked.shape[2]
    re_block = jnp.einsum("cfa,cfb->cab", row_block, stacked, preferred_element_type=jnp.float32)
    im_block = jnp.einsum("cfa,cfb->cab", row_block, rotated, preferred_element_type=jnp.float32)
    row_ids = vis_index * row_count + jnp.arange(row_count, dtype=jnp.int32)
    col_ids = jnp.arange(input_total, dtype=jnp.int32)
    contribution = jnp.where(col_ids[None, None, :] >= row_ids[None, :, None], re_block, im_block)
    return contribution


def per_device(samples, history, fir_taps, kept_channels):
    vis_count = lax.axis_size("vis")
    vis_index = lax.axis_index("vis")
    inp_count = lax.axis_size("inp")
    frame_count, input_count, sample_count = samples.shape
    history_len = TAPS - 1
    previous = shifted(samples[frame_count - history_len :], "vis", 1)
    previous = jnp.where(vis_index == 0, history, previous)
    extended = jnp.concatenate([previous, samples], axis=0)
    weighted = fir_taps[0][None, None, :] * extended[0:frame_count].astype(jnp.float32)
    for tap_index in range(1, TAPS):
        weighted = weighted + fir_taps[tap_index][None, None, :] * extended[
            tap_index : tap_index + frame_count
        ].astype(jnp.float32)
    weighted = weighted.astype(jnp.bfloat16)
    dft_table = make_table(kept_channels, sample_count)
    kept_total = kept_channels.shape[0]
    spectra = jnp.einsum(
        "kn,fin->kfi", dft_table, weighted, preferred_element_type=jnp.float32
    ).astype(jnp.bfloat16)
    spectra = spectra.reshape(2, kept_total, frame_count, input_count)
    input_total = input_count * inp_count
    row_count = input_total // vis_count
    frame_total = frame_count * vis_count
    initial = jnp.zeros((CH_DEV, row_count, input_total), jnp.float32)
    correlate = partial(add_frames, vis_index=vis_index, row_count=row_count)
    all_frames = lax.all_gather(spectra, "vis", axis=2, tiled=True)
    channel_data = lax.all_to_all(all_frames, "inp", split_axis=1, concat_axis=3, tiled=True)
    summed = correlate(initial, channel_data, 0)
    return (summed / float(frame_total)).astype(jnp.bfloat16)


def solution(mesh):
    return jax.shard_map(
        per_device,
        mesh=mesh,
        in_specs=(P("vis", "inp", None), P(None, "inp", None), P(), P()),
        out_specs=P("inp", "vis", None),
        check_vma=False,
    )
```

profile of v0, /device:TPU:1, one launch (start us, length us, event | category | flops | bytes accessed | tf_op | source)
XLA Modules:
  0.0 116.5 jit_solution(1827298505399509753)
XLA Ops:
  6.5 0.0 copy-start
  6.5 0.0 all-gather.2.cloned.1.call-start
  6.5 1.1 slice.33
  7.6 4.0 %collective-permute-start = (bf16[3,16,2048]{2,1,0:T(8,128)(2,1)S(1)}, bf16[3,16,2048]{2,1,0:T(8,128)(2,1)S(1)}, u32[]{:S(2)}, u32[]{:S(2)}) collective-permute-start(bf16[3,16,2048]{2,1,0:T(8,128)(2,1)S(1)} %slice.33), channel_id=1, source_target_pairs={{0,1},{1,2},{2,3},{4,5},{5,6},{6,7},{8,9},{9,10},{10,11},{12,13},{... | collective-permute-start | bytes 589832 | tf_op jit(solution)/shard_map/ppermute | solution.py:15
  11.6 5.6 %multiply_convert_fusion.2 = (bf16[128,2048]{1,0:T(8,128)(2,1)S(1)}, bf16[128,2048]{1,0:T(8,128)(2,1)S(1)}) fusion(s32[128]{0:T(128)} %param.7), kind=kLoop, calls=%fused_computation.33 | loop fusion | flops 4980736 | bytes 1049088 | tf_op jit(solution)/shard_map/convert
  17.2 1.5 %fusion.29 = (f32[1,2048]{1,0:T(1,128)S(1)}, f32[1,2048]{1,0:T(1,128)S(1)}, f32[1,2048]{1,0:T(1,128)}, f32[1,2048]{1,0:T(1,128)}) fusion(f32[4,2048]{1,0:T(4,128)} %param.6), kind=kLoop, calls=%fused_computation.46 | loop fusion | bytes 65536 | tf_op jit(solution)/shard_map/slice | solution.py:51
  18.8 0.0 collective-permute-done
  18.8 1.0 broadcast_select_fusion
  19.7 0.0 copy-done
  19.7 2.7 %add_convert_fusion = bf16[32,16,2048]{2,1,0:T(8,128)(2,1)S(1)} fusion(bf16[32,16,2048]{2,1,0:T(8,128)(2,1)S(1)} %copy-done, bf16[3,16,2048]{2,1,0:T(8,128)(2,1)S(1)} %broadcast_select_fusion, f32[2048]{0:T(1024)} %bitcast.36, f32[2048]{0:T(1024)} %bitcast.37, f32[2048]{0:T(1024)S(1)} %bitcast.35, f32[2048]{0:T(1024)S(1)} %bitcast.34), kind=kLoop, calls=%fused_computation.1 | loop fusion | flops 15728640 | bytes 4423680 | tf_op jit(solution)/shard_map/convert_element_type | solution.py:56
  22.5 1.6 %fusion.5 = bf16[256,32,16]{0,1,2:T(8,128)(2,1)S(1)} fusion(bf16[32,16,2048]{2,1,0:T(8,128)(2,1)S(1)} %add_convert_fusion, bf16[128,2048]{1,0:T(8,128)(2,1)S(1)} %get-tuple-element.12, bf16[128,2048]{1,0:T(8,128)(2,1)S(1)} %get-tuple-element.11), kind=kOutput, calls=%fused_computation.16 | convolution fusion | flops 539099136 | bytes 3407872 | tf_op jit(solution)/shard_map/kn,fin->kfi/dot_general | solution.py:59
  24.1 0.1 reshape.47
  24.2 1.0 copy.9
  25.2 0.0 all-gather.2.cloned.1.call-update
  25.2 32.2 %all-gather.2.cloned.1.call-done = bf16[2,128,128,16]{1,3,0,2:T(8,128)(2,1)} async-done(((bf16[2,128,32,16]{1,3,0,2:T(8,128)(2,1)}), bf16[2,128,128,16]{1,3,0,2:T(8,128)(2,1)}) %all-gather.2.cloned.1.call-update) | async-done | bytes 1048592 | tf_op jit(solution)/shard_map/all_gather | solution.py:68
  57.5 3.2 %copy.10 = bf16[2,128,128,16]{2,3,0,1:T(8,128)(2,1)} copy(bf16[2,128,128,16]{1,3,0,2:T(8,128)(2,1)} %all-gather.2.cloned.1.call-done) | data formatting | bytes 2097152 | tf_op jit(solution)/shard_map/all_gather | solution.py:68
  60.7 15.2 %all-to-all-start = ((bf16[2,128,128,16]{2,3,0,1:T(8,128)(2,1)}), bf16[2,128,128,16]{2,3,0,1:T(8,128)(2,1)S(1)}, u32[]{:S(2)}, u32[]{:S(2)}) async-start(bf16[2,128,128,16]{2,3,0,1:T(8,128)(2,1)} %copy.10), calls=%async_computation | async-start | bytes 2097152 | tf_op jit(solution)/shard_map/all_to_all | solution.py:69
  75.9 30.4 %all-to-all-done = bf16[2,128,128,16]{2,3,0,1:T(8,128)(2,1)S(1)} async-done(((bf16[2,128,128,16]{2,3,0,1:T(8,128)(2,1)}), bf16[2,128,128,16]{2,3,0,1:T(8,128)(2,1)S(1)}, u32[]{:S(2)}, u32[]{:S(2)}) %all-to-all-start) | async-done | bytes 1048608 | tf_op jit(solution)/shard_map/all_to_all | solution.py:69
  106.3 0.2 copy.17
  106.5 0.2 fusion.28
  106.7 0.1 bitcast_negate_fusion
  106.8 0.7 fusion.9
  107.5 2.1 %fusion = bf16[1,512,2048]{2,1,0:T(8,128)(2,1)} fusion(f32[512,2048]{1,0:T(8,128)S(1)} %fusion.9, s32[512]{0:T(512)S(1)} %iota_add_fusion, bf16[1,128,2048]{1,2,0:T(8,128)(2,1)S(1)} %bitcast.30, bf16[1,128,2048]{1,2,0:T(8,128)(2,1)S(1)} %bitcast_negate_fusion, s32[]{:T(128)S(6)} %select_n.26, bf16[1,128,2048]{1,2,0:T(8,128)(2,1)S(1)} %bitcast.32), kind=kOutput, calls=%fused_computation.5 | convolution fusion | flops 543686656 | bytes 8390660 | tf_op jit(solution)/shard_map/cfa,cfb->cab/dot_general | solution.py:35
  (1 shorter events, 0.0 us)
Async XLA Ops:
  6.5 13.2 %copy-start = (bf16[32,16,2048]{2,1,0:T(8,128)(2,1)S(1)}, bf16[32,16,2048]{2,1,0:T(8,128)(2,1)}, u32[]{:S(2)}) copy-start(bf16[32,16,2048]{2,1,0:T(8,128)(2,1)} %param.4) | copy-start | bytes 6291460
  6.5 50.9 %all-gather.2.cloned.1.call-start = ((), (), s32[]{:S(2)}) async-start(), calls=%async_computation.1 | async-start | bytes 1310720 | tf_op jit(solution)/shard_map/all_gather | solution.py:68
  7.6 11.1 %collective-permute-start = (bf16[3,16,2048]{2,1,0:T(8,128)(2,1)S(1)}, bf16[3,16,2048]{2,1,0:T(8,128)(2,1)S(1)}, u32[]{:S(2)}, u32[]{:S(2)}) collective-permute-start(bf16[3,16,2048]{2,1,0:T(8,128)(2,1)S(1)} %slice.33), channel_id=1, source_target_pairs={{0,1},{1,2},{2,3},{4,5},{5,6},{6,7},{8,9},{9,10},{10,11},{12,13},{... | collective-permute-start | bytes 589832 | tf_op jit(solution)/shard_map/ppermute | solution.py:15
  60.7 45.6 %all-to-all-start = ((bf16[2,128,128,16]{2,3,0,1:T(8,128)(2,1)}), bf16[2,128,128,16]{2,3,0,1:T(8,128)(2,1)S(1)}, u32[]{:S(2)}, u32[]{:S(2)}) async-start(bf16[2,128,128,16]{2,3,0,1:T(8,128)(2,1)} %copy.10), calls=%async_computation | async-start | bytes 2097152 | tf_op jit(solution)/shard_map/all_to_all | solution.py:69
Sparse Core Ops, SparseCore 0:
  25.4 32.0 all-gather.1
where the time goes:
time: 117 us
  waiting for transfers between devices  62.7 us (54%)
  starting transfers between devices  19.2 us (16%)
  between operations  13.5 us (12%)
  other arithmetic  9.41 us (8%)
  local copies, waits for them, and re-layouts  7.24 us (6%)
  matrix products  4.52 us (4%)
    all_gather x1, waiting for transfers between devices, per_device(): all_frames = lax.all_gather(spectra, 'vis', axis=2, tiled=True)  32.2 us
    all_to_all x1, waiting for transfers between devices, per_device(): lax.all_to_all(all_frames, 'inp', split_axis=1, concat_axis=3, tiled=True)  30.4 us
    all_to_all x1, starting transfers between devices, per_device(): lax.all_to_all(all_frames, 'inp', split_axis=1, concat_axis=3, tiled=True)  15.2 us
    another operation x1, other arithmetic  5.62 us
    ppermute x1, starting transfers between devices, shifted(): lax.ppermute(value, axis, [(source, source + steps) for source in range(i...  3.96 us
    all_gather x1, local copies, waits for them, and re-layouts, per_device(): all_frames = lax.all_gather(spectra, 'vis', axis=2, tiled=True)  3.17 us
    convert_element_type x1, other arithmetic, per_device(): weighted = weighted.astype(jnp.bfloat16)  2.74 us
  transfers between devices with their start and end apart: 3, of which 2 were waited for; matrix products, arithmetic and copies ran while one was open for 6% of the time, Pallas kernels for 0%

commit v1 on v0

--- a/solution.py
+++ b/solution.py
@@ -65,7 +65,16 @@
     frame_total = frame_count * vis_count
     initial = jnp.zeros((CH_DEV, row_count, input_total), jnp.float32)
     correlate = partial(add_frames, vis_index=vis_index, row_count=row_count)
-    all_frames = lax.all_gather(spectra, "vis", axis=2, tiled=True)
+    _use_ticks = lambda mine_x: jnp.concatenate(
+        jax.lax.all_to_all(
+            jnp.stack(jax.lax.axis_size("vis") * [mine_x], axis=0),
+            axis_name="vis",
+            split_axis=0,
+            concat_axis=0,
+        ),
+        axis=2,
+    )
+    all_frames = _use_ticks(spectra)
     channel_data = lax.all_to_all(all_frames, "inp", split_axis=1, concat_axis=3, tiled=True)
     summed = correlate(initial, channel_data, 0)
     return (summed / float(frame_total)).astype(jnp.bfloat16)

time: 117 us -> 90.2 us (0.77)
  waiting for transfers between devices: 62.7 us -> 30.4 us
  blocking collectives: 0 us -> 13.4 us
  between operations: 13.5 us -> 0.12 us
  starting transfers between devices: 19.2 us -> 26.1 us
  local copies, waits for them, and re-layouts: 7.24 us -> 5.84 us
    all_gather x1 -> x0, waiting for transfers between devices: 32.2 us -> none  [per_device(): all_frames = lax.all_gather(spectra, 'vis', axis=2, tiled=True)]
    all_to_all x0 -> x1, blocking collectives: none -> 13.4 us  [per_device(): jax.lax.all_to_all(jnp.stack(jax.lax.axis_size('vis') * [mine_x], axis=0)...]
    all_to_all x1, starting transfers between devices: 15.2 us -> 22.2 us  [per_device(): lax.all_to_all(all_frames, 'inp', split_axis=1, concat_axis=3, tiled=True)]
    all_gather x1 -> x0, local copies, waits for them, and re-layouts: 3.17 us -> none  [per_device(): all_frames = lax.all_gather(spectra, 'vis', axis=2, tiled=True)]
    reshape x2 -> x1, local copies, waits for them, and re-layouts: 1.08 us -> 2.26 us  [per_device(): jnp.concatenate(jax.lax.all_to_all(jnp.stack(jax.lax.axis_size('vis') * [...]
  transfers between devices with their start and end apart: 3 -> 2, of which waited for: 2 -> 1; matrix products, arithmetic and copies ran while one was open for 6% -> 8% of each run, Pallas kernels for 0% -> 0%
where the time goes in v1:
time: 90.2 us; the launch traced here: 89.8 us
  waiting for transfers between devices  30.4 us (34%)
  starting transfers between devices  26.1 us (29%)
  blocking collectives  13.4 us (15%)
  other arithmetic  9.42 us (10%)
  local copies, waits for them, and re-layouts  5.84 us (6%)
  matrix products  4.52 us (5%)
    all_to_all x1, waiting for transfers between devices, per_device(): lax.all_to_all(all_frames, 'inp', split_axis=1, concat_axis=3, tiled=True)  30.4 us
    all_to_all x1, starting transfers between devices, per_device(): lax.all_to_all(all_frames, 'inp', split_axis=1, concat_axis=3, tiled=True)  22.2 us
    all_to_all x1, blocking collectives, per_device(): jax.lax.all_to_all(jnp.stack(jax.lax.axis_size('vis') * [mine_x], axis=0)...  13.4 us
    another operation x1, other arithmetic  5.62 us
    ppermute x1, starting transfers between devices, shifted(): lax.ppermute(value, axis, [(source, source + steps) for source in range(i...  3.96 us
    convert_element_type x1, other arithmetic, per_device(): weighted = weighted.astype(jnp.bfloat16)  2.75 us
    reshape x1, local copies, waits for them, and re-layouts, per_device(): jnp.concatenate(jax.lax.all_to_all(jnp.stack(jax.lax.axis_size('vis') * [...  2.26 us
    dot_general x1, matrix products, add_frames(): jnp.einsum('cfa,cfb->cab', row_block, rotated, preferred_element_type=jnp...  2.14 us
  transfers between devices with their start and end apart: 2, of which 1 were waited for; matrix products, arithmetic and copies ran while one was open for 8% of the time, Pallas kernels for 0%

profile of v1, /device:TPU:1, one launch (start us, length us, event | category | flops | bytes accessed | tf_op | source)
XLA Modules:
  0.0 89.8 jit_solution(12733557642230645791)
XLA Ops:
  0.0 0.0 copy-start
  0.0 1.1 %slice.33 = bf16[3,16,2048]{2,1,0:T(8,128)(2,1)S(1)} slice(bf16[32,16,2048]{2,1,0:T(8,128)(2,1)} %param.4), slice={[29:32], [0:16], [0:2048]} | slice | bytes 393216 | tf_op jit(solution)/shard_map/slice | solution.py:48
  1.1 4.0 %collective-permute-start = (bf16[3,16,2048]{2,1,0:T(8,128)(2,1)S(1)}, bf16[3,16,2048]{2,1,0:T(8,128)(2,1)S(1)}, u32[]{:S(2)}, u32[]{:S(2)}) collective-permute-start(bf16[3,16,2048]{2,1,0:T(8,128)(2,1)S(1)} %slice.33), channel_id=1, source_target_pairs={{0,1},{1,2},{2,3},{4,5},{5,6},{6,7},{8,9},{9,10},{10,11},{12,13},{... | collective-permute-start | bytes 589832 | tf_op jit(solution)/shard_map/ppermute | solution.py:15
  5.1 5.6 %multiply_convert_fusion.2 = (bf16[128,2048]{1,0:T(8,128)(2,1)S(1)}, bf16[128,2048]{1,0:T(8,128)(2,1)S(1)}) fusion(s32[128]{0:T(128)} %param.7), kind=kLoop, calls=%fused_computation.33 | loop fusion | flops 4980736 | bytes 1049088 | tf_op jit(solution)/shard_map/convert
  10.7 1.6 %fusion.29 = (f32[1,2048]{1,0:T(1,128)S(1)}, f32[1,2048]{1,0:T(1,128)S(1)}, f32[1,2048]{1,0:T(1,128)}, f32[1,2048]{1,0:T(1,128)}) fusion(f32[4,2048]{1,0:T(4,128)} %param.6), kind=kLoop, calls=%fused_computation.46 | loop fusion | bytes 65536 | tf_op jit(solution)/shard_map/slice | solution.py:51
  12.3 0.0 collective-permute-done
  12.3 1.0 %broadcast_select_fusion = bf16[3,16,2048]{2,1,0:T(8,128)(2,1)S(1)} fusion(bf16[3,16,2048]{2,1,0:T(8,128)(2,1)} %param.5, bf16[3,16,2048]{2,1,0:T(8,128)(2,1)S(1)} %collective-permute-done, pred[]{:T(512)S(6)} %eq.5), kind=kLoop, calls=%fused_computation.39 | loop fusion | flops 98304 | bytes 589825 | tf_op jit(solution)/shard_map/jit(_where)/select_n | solution.py:49
  13.2 0.0 copy-done
  13.2 2.7 %add_convert_fusion = bf16[32,16,2048]{2,1,0:T(8,128)(2,1)S(1)} fusion(bf16[32,16,2048]{2,1,0:T(8,128)(2,1)S(1)} %copy-done, bf16[3,16,2048]{2,1,0:T(8,128)(2,1)S(1)} %broadcast_select_fusion, f32[2048]{0:T(1024)} %bitcast.40, f32[2048]{0:T(1024)} %bitcast.41, f32[2048]{0:T(1024)S(1)} %bitcast.39, f32[2048]{0:T(1024)S(1)} %bitcast.38), kind=kLoop, calls=%fused_computation.1 | loop fusion | flops 15728640 | bytes 4423680 | tf_op jit(solution)/shard_map/convert_element_type | solution.py:56
  16.0 1.6 %fusion.5 = bf16[256,32,16]{0,1,2:T(8,128)(2,1)S(1)} fusion(bf16[32,16,2048]{2,1,0:T(8,128)(2,1)S(1)} %add_convert_fusion, bf16[128,2048]{1,0:T(8,128)(2,1)S(1)} %get-tuple-element.12, bf16[128,2048]{1,0:T(8,128)(2,1)S(1)} %get-tuple-element.11), kind=kOutput, calls=%fused_computation.16 | convolution fusion | flops 539099136 | bytes 3407872 | tf_op jit(solution)/shard_map/kn,fin->kfi/dot_general | solution.py:59
  17.6 0.1 stack_reshape.2
  17.7 0.2 copy.17
  17.9 0.1 stack.3
  18.0 13.4 %all_to_all.20 = bf16[4,2,128,32,16]{2,4,3,1,0:T(8,128)(2,1)S(1)} all-to-all(bf16[4,2,128,32,16]{2,4,3,1,0:T(8,128)(2,1)S(1)} %stack.3), channel_id=1, replica_groups=mesh['inp'=128,'vis'=4] {'vis'}, dimensions={0} | all-to-all | bytes 2097152 | tf_op jit(solution)/shard_map/all_to_all | solution.py:69
  31.4 0.2 copy.18
  31.6 2.3 %copy.19 = bf16[2,128,128,16]{2,3,0,1:T(8,128)(2,1)} copy(bf16[2,128,128,16]{1,3,2,0:T(8,128)(2,1)S(1)} %bitcast.37) | data formatting | bytes 2097152 | tf_op jit(solution)/shard_map/reshape | solution.py:68
  33.8 22.2 %all-to-all-start.1 = ((bf16[2,128,128,16]{2,3,0,1:T(8,128)(2,1)}), bf16[2,128,128,16]{2,3,0,1:T(8,128)(2,1)S(1)}, u32[]{:S(2)}, u32[]{:S(2)}) async-start(bf16[2,128,128,16]{2,3,0,1:T(8,128)(2,1)} %copy.19), calls=%async_computation.1 | async-start | bytes 2097152 | tf_op jit(solution)/shard_map/all_to_all | solution.py:78
  56.0 30.4 %all-to-all-done.1 = bf16[2,128,128,16]{2,3,0,1:T(8,128)(2,1)S(1)} async-done(((bf16[2,128,128,16]{2,3,0,1:T(8,128)(2,1)}), bf16[2,128,128,16]{2,3,0,1:T(8,128)(2,1)S(1)}, u32[]{:S(2)}, u32[]{:S(2)}) %all-to-all-start.1) | async-done | bytes 1048608 | tf_op jit(solution)/shard_map/all_to_all | solution.py:78
  86.5 0.2 copy.26
  86.7 0.2 fusion.28
  86.8 0.1 bitcast_negate_fusion
  87.0 0.7 fusion.9
  87.7 2.1 %fusion = bf16[1,512,2048]{2,1,0:T(8,128)(2,1)} fusion(f32[512,2048]{1,0:T(8,128)S(1)} %fusion.9, s32[512]{0:T(512)S(1)} %iota_add_fusion, bf16[1,128,2048]{1,2,0:T(8,128)(2,1)S(1)} %bitcast.33, bf16[1,128,2048]{1,2,0:T(8,128)(2,1)S(1)} %bitcast_negate_fusion, s32[]{:T(128)S(6)} %select_n.26, bf16[1,128,2048]{1,2,0:T(8,128)(2,1)S(1)} %bitcast.35), kind=kOutput, calls=%fused_computation.5 | convolution fusion | flops 543686656 | bytes 8390660 | tf_op jit(solution)/shard_map/cfa,cfb->cab/dot_general | solution.py:35
  (1 shorter events, 0.0 us)
Async XLA Ops:
  0.0 13.2 %copy-start = (bf16[32,16,2048]{2,1,0:T(8,128)(2,1)S(1)}, bf16[32,16,2048]{2,1,0:T(8,128)(2,1)}, u32[]{:S(2)}) copy-start(bf16[32,16,2048]{2,1,0:T(8,128)(2,1)} %param.4) | copy-start | bytes 6291460
  1.1 11.2 %collective-permute-start = (bf16[3,16,2048]{2,1,0:T(8,128)(2,1)S(1)}, bf16[3,16,2048]{2,1,0:T(8,128)(2,1)S(1)}, u32[]{:S(2)}, u32[]{:S(2)}) collective-permute-start(bf16[3,16,2048]{2,1,0:T(8,128)(2,1)S(1)} %slice.33), channel_id=1, source_target_pairs={{0,1},{1,2},{2,3},{4,5},{5,6},{6,7},{8,9},{9,10},{10,11},{12,13},{... | collective-permute-start | bytes 589832 | tf_op jit(solution)/shard_map/ppermute | solution.py:15
  33.8 52.6 %all-to-all-start.1 = ((bf16[2,128,128,16]{2,3,0,1:T(8,128)(2,1)}), bf16[2,128,128,16]{2,3,0,1:T(8,128)(2,1)S(1)}, u32[]{:S(2)}, u32[]{:S(2)}) async-start(bf16[2,128,128,16]{2,3,0,1:T(8,128)(2,1)} %copy.19), calls=%async_computation.1 | async-start | bytes 2097152 | tf_op jit(solution)/shard_map/all_to_all | solution.py:78
